TPU v7x, 32 devices: a whole 2x2x4 slice. The times are simulated.
32 devices in a mesh: rep: 8 (over z, x), shard: 4 (over y, core).
Axes of the slice: x: 2, y: 2, z: 4, core: 2. Of those that a mesh axis runs over, the one named last changes fastest.
Arguments:
- tokens: bfloat16 [16384, 1024], P(('rep', 'shard')), may hold values from -6 to 6
- positions: int32 [16384], P(('rep', 'shard')), may hold values from 0 to 511, as said below
- lengths: int32 [64], replicated, may hold values from 0 to 512, as said below
- owner: int32 [64], replicated, may hold values from 0 to 31, as said below
- qkv_weight: bfloat16 [1024, 3072], P('shard'), may hold values from -0.1875 to 0.1875
- out_weight: bfloat16 [1024, 1024], P('shard'), may hold values from -1.5 to 1.5
- in_weight: bfloat16 [1024, 4096], P('shard'), may hold values from -0.1875 to 0.1875
- in_bias: bfloat16 [4096], P('shard'), may hold values from -3 to 3
- fc_weight: bfloat16 [4096, 1024], P('shard'), may hold values from -0.09375 to 0.09375
- fc_bias: bfloat16 [1024], P('shard'), may hold values from -3 to 3
- norm_gain: bfloat16 [1024], P('shard'), may hold values from 0.25 to 1.75
- norm_bias: bfloat16 [1024], P('shard'), may hold values from -2 to 2
- cotangent: bfloat16 [16384, 1024], P(('rep', 'shard')), may hold values from -6 to 6
Outputs:
- layer_out: bfloat16 [16384, 1024], P(('rep', 'shard'))
- input_grad: bfloat16 [16384, 1024], P(('rep', 'shard'))
- grad_qkv: float32 [1024, 3072], P('shard')
- grad_out: float32 [1024, 1024], P('shard')
- grad_in: float32 [1024, 4096], P('shard')
- grad_in_bias: float32 [4096], P('shard')
- grad_fc: float32 [4096, 1024], P('shard')
- grad_fc_bias: float32 [1024], P('shard')
- grad_gain: float32 [1024], P('shard')
- grad_norm_bias: float32 [1024], P('shard')
Inputs may be any that keep to these rules, and one draw needn't show every extreme that they name: Sequences 2 i and 2 i + 1 go to one device; their lengths sum to at most 512; some sequence has exactly 512 tokens; a length may be 0. Sequences 2 i and 2 i + 1 have the same owner, and every device owns exactly one such pair. `positions`: a token's position within its sequence, with the sequences packed as the steps say; unused slots hold 0.
All inputs are finite; a program needn't handle non-finite values.
Results may differ from a plain program's by a relative error of at most 0.011.
Values may be sent and summed in bfloat16 or wider, within the bound.
A program may use at most 256 MiB of HBM per device.

v0:
```python
from functools import partial
import math

import jax
import jax.numpy as jnp
from jax import lax
from jax.sharding import PartitionSpec as P

D = 1024
HEADS = 16
HEAD_DIM = 64
ROT_DIM = 32
TOK_DEV = 512


EPS = 1e-05
NEG = -1000000000.0
SCORE_SCALE = 0.125


def layout(lengths, owner, device):
    owned_mask = (owner == device).astype(jnp.int32)
    seq_ends = jnp.cumsum(lengths * owned_mask)
    seq_load = jnp.sum(lengths * owned_mask)
    slot_index = jnp.arange(TOK_DEV, dtype=jnp.int32)
    passed = (seq_ends[None, :] <= slot_index[:, None]) & (owned_mask[None, :] > 0)
    segment = jnp.sum(passed.astype(jnp.int32), axis=1)
    in_use = slot_index < seq_load
    return (jnp.where(in_use, segment, TOK_DEV + slot_index), in_use)


def layer_norm(inputs, scale_gain, norm_shift):
    center = inputs - jnp.mean(inputs, axis=-1, keepdims=True)
    spread = jnp.mean(center * center, axis=-1, keepdims=True)
    return center * lax.rsqrt(spread + EPS) * scale_gain + norm_shift


def rotary_tables(positions):
    freq_index = jnp.arange(ROT_DIM // 2, dtype=jnp.float32)
    inverse = jnp.exp(freq_index * (-2.0 * math.log(10000.0) / ROT_DIM))
    angles = positions.astype(jnp.float32)[:, None] * inverse[None, :]
    return (jnp.cos(angles), jnp.sin(angles))


def rotate(field, cosine, sine_table):
    row_count = field.shape[0]
    head_count = field.shape[1]
    turned = field[..., :ROT_DIM].reshape(row_count, head_count, ROT_DIM // 2, 2)
    first_half = turned[..., 0]
    second_half = turned[..., 1]
    cos_wide = cosine[:, None, :]
    sin_wide = sine_table[:, None, :]
    joined = jnp.stack(
        [
            first_half * cos_wide - second_half * sin_wide,
            second_half * cos_wide + first_half * sin_wide,
        ],
        -1,
    )
    return jnp.concatenate(
        [joined.reshape(row_count, head_count, ROT_DIM), field[..., ROT_DIM:]], -1
    )


def block_scores(query_block, key_block, allowed_block):
    raw_scores = (
        jnp.einsum("qhd,khd->hqk", query_block, key_block, preferred_element_type=jnp.float32)
        * SCORE_SCALE
    )
    return jnp.where(allowed_block[None], raw_scores, NEG)


def attend(queries, key_rows, value_rows, allowed):
    row_count = queries.shape[0]
    head_count = queries.shape[1]
    block_rows = min(512, row_count)
    group_size = min(8, head_count)
    head_parts = []
    norm_parts = []
    for head_start in range(0, head_count, group_size):
        head_end = head_start + group_size
        scores = block_scores(
            queries[0:block_rows, head_start:head_end], key_rows[:, head_start:head_end], allowed
        )
        row_peak = jnp.max(scores, axis=-1, keepdims=True)
        exponent = jnp.exp(scores - row_peak)
        row_total = jnp.sum(exponent, axis=-1, keepdims=True)
        soft_weights = (exponent / row_total).astype(jnp.bfloat16)
        row_parts = jnp.einsum(
            "hqk,khd->qhd",
            soft_weights,
            value_rows[:, head_start:head_end],
            preferred_element_type=jnp.float32,
        )
        row_norms = (row_peak + jnp.log(row_total))[..., 0]
        head_parts.append(row_parts)
        norm_parts.append(row_norms)
    return (jnp.concatenate(head_parts, 1), jnp.concatenate(norm_parts, 0))


def attend_back(queries, key_rows, value_rows, grad_attended, log_norm, allowed):
    row_count = queries.shape[0]
    head_count = queries.shape[1]
    block_rows = min(512, row_count)
    group_size = min(8, head_count)
    query_parts = []
    key_parts = []
    value_parts = []
    for head_start in range(0, head_count, group_size):
        head_end = head_start + group_size
        key_block = key_rows[:, head_start:head_end]
        value_block = value_rows[:, head_start:head_end]
        query_block = queries[0:block_rows, head_start:head_end]
        grad_block = grad_attended[0:block_rows, head_start:head_end]
        scores = block_scores(query_block, key_block, allowed)
        soft_full = jnp.exp(scores - log_norm[head_start:head_end, 0:block_rows][..., None])
        soft_low = soft_full.astype(jnp.bfloat16)
        grad_soft = jnp.einsum(
            "qhd,khd->hqk", grad_block, value_block, preferred_element_type=jnp.float32
        )
        row_delta = jnp.sum(soft_full * grad_soft, axis=-1, keepdims=True)
        grad_scores = (soft_full * (grad_soft - row_delta)).astype(jnp.bfloat16)
        row_parts = (
            jnp.einsum("hqk,khd->qhd", grad_scores, key_block, preferred_element_type=jnp.float32)
            * SCORE_SCALE
        )
        key_sum = (
            jnp.einsum("hqk,qhd->khd", grad_scores, query_block, preferred_element_type=jnp.float32)
            * SCORE_SCALE
        )
        value_sum = jnp.einsum(
            "hqk,qhd->khd", soft_low, grad_block, preferred_element_type=jnp.float32
        )
        query_parts.append(row_parts)
        key_parts.append(key_sum)
        value_parts.append(value_sum)
    return (
        jnp.concatenate(query_parts, 1),
        jnp.concatenate(key_parts, 1),
        jnp.concatenate(value_parts, 1),
    )


def body(
    tokens,
    positions,
    lengths,
    owner,
    qkv_weight,
    out_weight,
    in_weight,
    in_bias,
    fc_weight,
    fc_bias,
    norm_gain,
    norm_bias,
    cotangent,
):
    device = lax.axis_index(("rep", "shard"))
    segment, in_use = layout(lengths, owner, device)
    row_count = tokens.shape[0]
    slot_index = jnp.arange(row_count, dtype=jnp.int32)
    allowed = (segment[:, None] == segment[None, :]) & (slot_index[None, :] <= slot_index[:, None])
    gathered = (
        lax.all_gather(qkv_weight, "shard", axis=0, tiled=True),
        lax.all_gather(out_weight, "shard", axis=0, tiled=True),
        lax.all_gather(in_weight, "shard", axis=0, tiled=True),
        lax.all_gather(in_bias, "shard", axis=0, tiled=True),
        lax.all_gather(fc_weight, "shard", axis=0, tiled=True),
        lax.all_gather(fc_bias, "shard", axis=0, tiled=True),
        lax.all_gather(norm_gain, "shard", axis=0, tiled=True),
        lax.all_gather(norm_bias, "shard", axis=0, tiled=True),
    )
    qkv_full, out_full, in_full, in_bias_full, fc_full, fc_bias_full, gain_full, shift_full = (
        gathered
    )
    inputs = tokens.astype(jnp.float32)
    normed = layer_norm(
        inputs, gain_full.astype(jnp.float32), shift_full.astype(jnp.float32)
    ).astype(jnp.bfloat16)
    merged_rows = jnp.dot(normed, qkv_full, preferred_element_type=jnp.float32)
    cosine, sine_table = rotary_tables(positions)
    queries = rotate(
        merged_rows[:, :D].reshape(row_count, HEADS, HEAD_DIM), cosine, sine_table
    ).astype(jnp.bfloat16)
    key_rows = rotate(
        merged_rows[:, D : 2 * D].reshape(row_count, HEADS, HEAD_DIM), cosine, sine_table
    ).astype(jnp.bfloat16)
    value_rows = merged_rows[:, 2 * D :].reshape(row_count, HEADS, HEAD_DIM).astype(jnp.bfloat16)
    attended, log_norm = attend(queries, key_rows, value_rows, allowed)
    attended_low = attended.reshape(row_count, D).astype(jnp.bfloat16)
    hidden = jnp.dot(normed, in_full, preferred_element_type=jnp.float32) + in_bias_full.astype(
        jnp.float32
    )
    active = jax.nn.gelu(hidden, approximate=True).astype(jnp.bfloat16)
    branch_attn = jnp.dot(attended_low, out_full, preferred_element_type=jnp.float32)
    branch_mlp = jnp.dot(active, fc_full, preferred_element_type=jnp.float32) + fc_bias_full.astype(
        jnp.float32
    )
    layer_out = (inputs + branch_attn + branch_mlp).astype(jnp.bfloat16)
    regathered = (
        lax.all_gather(qkv_weight, "shard", axis=0, tiled=True),
        lax.all_gather(out_weight, "shard", axis=0, tiled=True),
        lax.all_gather(in_weight, "shard", axis=0, tiled=True),
        lax.all_gather(fc_weight, "shard", axis=0, tiled=True),
        lax.all_gather(norm_gain, "shard", axis=0, tiled=True),
        lax.all_gather(norm_bias, "shard", axis=0, tiled=True),
    )
    qkv_back, out_back, in_back, fc_back, gain_back, shift_back = regathered
    upstream = cotangent * in_use[:, None].astype(jnp.bfloat16)
    grad_fc = jnp.einsum("tf,td->fd", active, upstream, preferred_element_type=jnp.float32)
    grad_fc_bias = jnp.sum(upstream.astype(jnp.float32), axis=0)
    grad_out = jnp.einsum("te,td->ed", attended_low, upstream, preferred_element_type=jnp.float32)
    grad_active = jnp.einsum("td,fd->tf", upstream, fc_back, preferred_element_type=jnp.float32)
    hidden_out, gelu_back = jax.vjp(partial(jax.nn.gelu, approximate=True), hidden)
    grad_hidden = gelu_back(grad_active)[0].astype(jnp.bfloat16)
    grad_in = jnp.einsum("td,tf->df", normed, grad_hidden, preferred_element_type=jnp.float32)
    grad_in_bias = jnp.sum(grad_hidden.astype(jnp.float32), axis=0)
    grad_attended = (
        jnp.einsum("td,ed->te", upstream, out_back, preferred_element_type=jnp.float32)
        .astype(jnp.bfloat16)
        .reshape(row_count, HEADS, HEAD_DIM)
    )
    grad_queries, grad_keys, grad_values = attend_back(
        queries, key_rows, value_rows, grad_attended, log_norm, allowed
    )
    query_back = rotate(
        grad_queries.astype(jnp.bfloat16).astype(jnp.float32), cosine, -sine_table
    ).reshape(row_count, D)
    key_back = rotate(
        grad_keys.astype(jnp.bfloat16).astype(jnp.float32), cosine, -sine_table
    ).reshape(row_count, D)
    grad_merged = jnp.concatenate(
        [query_back, key_back, grad_values.reshape(row_count, D)], -1
    ).astype(jnp.bfloat16)
    grad_qkv = jnp.einsum("td,te->de", normed, grad_merged, preferred_element_type=jnp.float32)
    grad_normed = jnp.einsum(
        "te,de->td", grad_merged, qkv_back, preferred_element_type=jnp.float32
    ) + jnp.einsum("tf,df->td", grad_hidden, in_back, preferred_element_type=jnp.float32)
    normed_again, norm_back = jax.vjp(
        layer_norm, inputs, gain_back.astype(jnp.float32), shift_back.astype(jnp.float32)
    )
    grad_inputs, grad_gain, grad_shift = norm_back(grad_normed)
    input_grad = (grad_inputs + upstream.astype(jnp.float32)).astype(jnp.bfloat16)
    rep_count = lax.axis_size("rep")
    shard_count = lax.axis_size("shard")
    grad_scale = 1.0 / math.sqrt(TOK_DEV * rep_count * shard_count)
    grad_qkv = grad_qkv * grad_scale
    grad_out = grad_out * grad_scale
    grad_in = grad_in * grad_scale
    grad_in_bias = grad_in_bias * grad_scale
    grad_fc = grad_fc * grad_scale
    grad_fc_bias = grad_fc_bias * grad_scale
    grad_gain = grad_gain * grad_scale
    grad_shift = grad_shift * grad_scale
    owner_sums = (
        lax.psum_scatter(grad_qkv, "shard", scatter_dimension=0, tiled=True),
        lax.psum_scatter(grad_out, "shard", scatter_dimension=0, tiled=True),
        lax.psum_scatter(grad_in, "shard", scatter_dimension=0, tiled=True),
        lax.psum_scatter(grad_in_bias, "shard", scatter_dimension=0, tiled=True),
        lax.psum_scatter(grad_fc, "shard", scatter_dimension=0, tiled=True),
        lax.psum_scatter(grad_fc_bias, "shard", scatter_dimension=0, tiled=True),
        lax.psum_scatter(grad_gain, "shard", scatter_dimension=0, tiled=True),
        lax.psum_scatter(grad_shift, "shard", scatter_dimension=0, tiled=True),
    )
    summed = lax.psum(
        (
            owner_sums[0],
            owner_sums[1],
            owner_sums[2],
            owner_sums[3],
            owner_sums[4],
            owner_sums[5],
            owner_sums[6],
            owner_sums[7],
        ),
        "rep",
    )
    return (
        layer_out,
        input_grad,
        summed[0],
        summed[1],
        summed[2],
        summed[3],
        summed[4],
        summed[5],
        summed[6],
        summed[7],
    )


def solution(mesh):
    in_specs = (
        P(("rep", "shard"), None),
        P(("rep", "shard")),
        P(),
        P(),
        P("shard", None),
        P("shard", None),
        P("shard", None),
        P("shard"),
        P("shard", None),
        P("shard"),
        P("shard"),
        P("shard"),
        P(("rep", "shard"), None),
    )
    out_specs = (
        P(("rep", "shard"), None),
        P(("rep", "shard"), None),
        P("shard", None),
        P("shard", None),
        P("shard", None),
        P("shard"),
        P("shard", None),
        P("shard"),
        P("shard"),
        P("shard"),
    )
    return jax.shard_map(body, mesh=mesh, in_specs=in_specs, out_specs=out_specs, check_vma=False)
```

profile of v0, /device:TPU:0, one launch (start us, length us, event | category | flops | bytes accessed | tf_op | source)
XLA Modules:
  0.0 1024.6 jit_solution(16834042041016692255)
XLA Ops:
  10.2 6.0 all-gather.1
  16.2 5.4 all-gather
  25.6 9.3 all-gather.10.cloned.1.call-done
  34.9 2.9 convolution_convert_fusion
  38.4 44.5 %all-gather.8.cloned.1.call-done = bf16[1024,3072]{1,0:T(8,128)(2,1)} async-done(((bf16[256,3072]{1,0:T(8,128)(2,1)}), bf16[1024,3072]{1,0:T(8,128)(2,1)}) %all-gather.8.cloned.1.call-update) | async-done | bytes 6291472 | tf_op jit(solution)/shard_map/all_gather | solution.py:165
  82.9 5.7 fusion.98
  89.8 2.3 fusion.101
  92.1 3.2 copy.90
  95.3 2.4 slice.203
  97.7 2.3 slice.123
  100.0 2.9 copy.93
  102.9 2.1 slice.202
  105.0 2.3 slice.128
  107.3 1.7 copy.88
  108.9 1.8 copy.91
  110.8 1.8 copy.94
  124.0 3.4 convolution_multiply_fusion.2
  127.5 5.3 multiply_reduce_fusion
  133.5 3.9 multiply_convert_fusion
  137.5 3.0 fusion.59
  140.5 2.3 multiply_reduce_fusion.1
  142.8 3.9 multiply_convert_fusion.1
  146.7 3.1 fusion.60
  160.5 9.6 convolution_multiply_fusion.1
  170.8 5.3 all_gather.34
  176.2 7.4 fusion.96
  183.6 3.2 copy-done.37
  186.8 10.1 broadcast_multiply_fusion
  197.0 5.5 all-gather.14.cloned.1.call-done
  202.5 13.3 %convert_reduce_fusion = (f32[4096]{0:T(1024)S(1)}, bf16[512,4096]{1,0:T(8,128)(2,1)S(1)}) fusion(f32[512,4096]{1,0:T(8,128)} %copy-done.37, f32[4096]{0:T(1024)S(1)} %convert_element_type.102, bf16[4096,1024]{1,0:T(8,128)(2,1)} %all-gather.14.cloned.1.call-done, bf16[512,1024]{1,0:T(8,128)(2,1)} %param.25, bf16[512]{0:T(512)(128)(2,1)S(1)} %fusion.80), kind=kOutput, calls=%fused_computation.11 | convolution fusion | flops 4343721984 | bytes 22053888 | tf_op jit(solution)/shard_map/td,fd->tf/dot_general | solution.py:214
  215.8 2.0 copy-done.36
  217.8 8.7 convolution_multiply_fusion
  226.6 22.9 %reduce-scatter.7.cloned.1.call-done = f32[256,1024]{1,0:T(8,128)} async-done(((f32[1024,1024]{1,0:T(8,128)}), f32[256,1024]{1,0:T(8,128)}) %reduce-scatter.7.cloned.1.call-update) | async-done | bytes 1048592 | tf_op jit(solution)/shard_map/reduce_scatter | solution.py:258
  249.5 102.1 %reduce-scatter.5.cloned.1.call-done = f32[256,3072]{1,0:T(8,128)} async-done(((f32[1024,3072]{1,0:T(8,128)}), f32[256,3072]{1,0:T(8,128)}) %reduce-scatter.5.cloned.1.call-update) | async-done | bytes 3145744 | tf_op jit(solution)/shard_map/reduce_scatter | solution.py:257
  351.5 127.7 %reduce-scatter.11.cloned.1.call-done = f32[1024,1024]{1,0:T(8,128)} async-done(((f32[4096,1024]{1,0:T(8,128)}), f32[1024,1024]{1,0:T(8,128)}) %reduce-scatter.11.cloned.1.call-update) | async-done | bytes 4194320 | tf_op jit(solution)/shard_map/reduce_scatter | solution.py:261
  479.2 127.7 %reduce-scatter.9.cloned.1.call-done = f32[256,4096]{1,0:T(8,128)} async-done(((f32[1024,4096]{1,0:T(8,128)}), f32[256,4096]{1,0:T(8,128)}) %reduce-scatter.9.cloned.1.call-update) | async-done | bytes 4194320 | tf_op jit(solution)/shard_map/reduce_scatter | solution.py:259
  609.4 5.1 all-gather.2
  614.5 9.5 fusion.104
  624.0 6.8 fusion.100
  631.9 1.9 convert_reduce_fusion.2
  633.9 11.3 %all-reduce.6 = (f32[4096]{0:T(1024)S(1)}, f32[1024]{0:T(1024)S(1)}, f32[1024]{0:T(1024)S(1)}, f32[1024]{0:T(1024)S(1)}) all-reduce(f32[4096]{0:T(1024)S(1)} %broadcast_multiply_fusion.2, f32[1024]{0:T(1024)S(1)} %broadcast_multiply_fusion.5, ...), channel_id=5, replica_groups=mesh['rep'=8,'shard'=4] {'shard'}, use_global_device_ids=true, to_apply=%region_20.21.clone | all-reduce | flops 7168 | bytes 57344
  645.4 23.6 %all-reduce.4 = (f32[1024]{0:T(1024)}, f32[256]{0:T(256)}, f32[256]{0:T(256)}, f32[256]{0:T(256)}) all-reduce(f32[1024]{0:T(1024)S(1)} %dynamic-slice.1, f32[256]{0:T(256)S(1)} %dynamic-slice.3, f32[256]{0:T(256)S(1)} %dynamic-slice.5, f32[256]{0:T(256)S(1)} %dynamic-slice.7), channel_id=1, replica_groups=mesh['rep'=8,'shard'=4] {'rep'}, use_global_device_ids=true, to_apply=%region_21.22 | all-reduce | flops 1792 | bytes 14336 | tf_op jit(solution)/shard_map/psum | solution.py:266
  669.0 10.6 %fusion.93 = f32[512,1024]{1,0:T(8,128)S(1)} fusion(bf16[4096,1024]{1,0:T(8,128)(2,1)} %all-gather.14.cloned.1.call-done, f32[512,4096]{1,0:T(8,128)} %copy-done.37, f32[4096]{0:T(1024)S(1)} %convert_element_type.102), kind=kOutput, calls=%fused_computation.163 | convolution fusion | flops 4315938816 | bytes 18890752 | tf_op jit(solution)/shard_map/dot_general | solution.py:197
  679.7 2.4 fusion.32
  682.1 325.0 %all-reduce.9.cloned.1.call-done = (f32[256,3072]{1,0:T(8,128)}, f32[256,1024]{1,0:T(8,128)}, f32[256,4096]{1,0:T(8,128)}, f32[1024,1024]{1,0:T(8,128)}) async-done(((f32[256,3072]{1,0:T(8,128)}, f32[256,1024]{1,0:T(8,128)}, f32[256,4096]{1,0:T(8,128)}, f32[1024,1024]{1,0:T(8,128)}), (f32[256,3072]{1,0:T(8,128)}, f32[256,1024]{1,0:T(8,128)}, f32[256,4096]{1,0:T(8,128)}, ...) | async-done | bytes 12582928 | tf_op jit(solution)/shard_map/psum | solution.py:266
  1007.0 4.0 copy.129
  1012.0 2.1 copy.131
  1015.7 2.0 copy.132
  (170 shorter events, 36.9 us)
Async XLA Ops:
  7.2 2.9 copy-start.32
  7.2 2.9 copy-start.33
  7.2 2.9 copy-start.28
  7.2 14.4 %copy-start.30 = (s32[64]{0:T(128)S(1)}, s32[64]{0:T(128)}, u32[]{:S(2)}) copy-start(s32[64]{0:T(128)} %param.16) | copy-start | bytes 772
  7.2 14.4 %copy-start.29 = (s32[64]{0:T(128)S(1)}, s32[64]{0:T(128)}, u32[]{:S(2)}) copy-start(s32[64]{0:T(128)} %param.15) | copy-start | bytes 772
  7.2 16.1 %copy-start.2 = (bf16[512,1024]{1,0:T(8,128)(2,1)S(1)}, bf16[512,1024]{1,0:T(8,128)(2,1)}, u32[]{:S(2)}) copy-start(bf16[512,1024]{1,0:T(8,128)(2,1)} %param.13) | copy-start | bytes 3145732
  7.2 27.7 %all-gather.10.cloned.1.call-start = ((), (), s32[]{:S(2)}) async-start(), calls=%async_computation.5 | async-start | bytes 2621440 | tf_op jit(solution)/shard_map/all_gather | solution.py:166
  8.0 27.0 %copy-start.12 = (bf16[512,1024]{1,0:T(8,128)(2,1)S(1)}, bf16[512,1024]{1,0:T(8,128)(2,1)}, u32[]{:S(2)}) copy-start(bf16[512,1024]{1,0:T(8,128)(2,1)} %param.25) | copy-start | bytes 3145732
  8.0 74.9 %all-gather.8.cloned.1.call-start = ((), (), s32[]{:S(2)}) async-start(), calls=%async_computation.4 | async-start | bytes 7864320 | tf_op jit(solution)/shard_map/all_gather | solution.py:165
  8.7 167.4 %all-gather.12.cloned.1.call-start = ((), (), s32[]{:S(2)}) async-start(), calls=%async_computation.6 | async-start | bytes 10485760 | tf_op jit(solution)/shard_map/all_gather | solution.py:167
  9.5 193.0 %all-gather.14.cloned.1.call-start = ((), (), s32[]{:S(2)}) async-start(), calls=%async_computation.7 | async-start | bytes 10485760 | tf_op jit(solution)/shard_map/all_gather | solution.py:169
  10.0 239.4 %reduce-scatter.7.cloned.1.call-start = ((), (), s32[]{:S(2)}) async-start(), calls=%async_computation.9 | async-start | bytes 5242880 | tf_op jit(solution)/shard_map/reduce_scatter | solution.py:258
  112.6 1.1 copy-start.16
  112.6 1.2 copy-start.18
  113.4 3.2 copy-start.20
  113.8 2.8 copy-start.22
  115.4 4.0 copy-start
  118.2 3.2 copy-start.1
  121.4 2.6 copy-start.13
  123.1 1.0 copy-start.7
  127.5 224.1 %reduce-scatter.5.cloned.1.call-start = ((), (), s32[]{:S(2)}) async-start(), calls=%async_computation.8 | async-start | bytes 15728640 | tf_op jit(solution)/shard_map/reduce_scatter | solution.py:257
  127.5 5.3 slice-start.2
  127.5 6.0 slice-start.3
  127.5 12.9 %slice-start = ((s8[8388608]{0:T(1024)(128)(4,1)}), s8[4194304]{0:T(1024)(128)(4,1)S(1)}, s32[]{:S(2)}) async-start(s8[8388608]{0:T(1024)(128)(4,1)} %bitcast.60), calls=%async_computation.13 | async-start | bytes 8388608
  133.5 3.9 copy-start.19
  133.5 3.9 copy-start.23
  133.5 7.0 slice-start.1
  142.8 3.9 copy-start.24
  146.7 3.9 copy-start.3
  149.8 1.2 copy-start.17
  149.8 1.4 copy-start.21
  151.3 2.9 copy-start.4
  157.5 3.0 copy-start.10
  170.2 309.0 %reduce-scatter.11.cloned.1.call-start = ((), (), s32[]{:S(2)}) async-start(), calls=%async_computation.11 | async-start | bytes 20971520 | tf_op jit(solution)/shard_map/reduce_scatter | solution.py:261
  176.2 10.7 %copy-start.14 = (bf16[512,1024]{1,0:T(8,128)(2,1)S(1)}, bf16[512,1024]{1,0:T(8,128)(2,1)}, u32[]{:S(2)}) copy-start(bf16[512,1024]{1,0:T(8,128)(2,1)} %param.25) | copy-start | bytes 3145732
  183.6 3.2 copy-start.37
  197.0 409.9 %reduce-scatter.9.cloned.1.call-start = ((), (), s32[]{:S(2)}) async-start(), calls=%async_computation.10 | async-start | bytes 20971520 | tf_op jit(solution)/shard_map/reduce_scatter | solution.py:259
  215.8 2.0 copy-start.36
  226.5 780.5 %all-reduce.9.cloned.1.call-start = ((), (), s32[]{:S(2)}) async-start(), calls=%async_computation.12 | async-start | bytes 25165824 | tf_op jit(solution)/shard_map/psum | solution.py:266
  606.9 2.5 copy-start.34
  614.5 9.5 copy-start.11
  624.0 6.9 copy-start.26
  624.0 7.9 copy-start.15
  669.0 10.6 %copy-start.8 = (bf16[512,16,64]{0,2,1:T(8,128)(2,1)S(1)}, bf16[512,16,64]{0,2,1:T(8,128)(2,1)}, u32[]{:S(2)}) copy-start(bf16[512,16,64]{0,2,1:T(8,128)(2,1)} %copy-done.7) | copy-start | bytes 3145732
  669.0 10.6 %copy-start.31 = (bf16[1024,1024]{1,0:T(8,128)(2,1)S(1)}, bf16[1024,1024]{1,0:T(8,128)(2,1)}, u32[]{:S(2)}) copy-start(bf16[1024,1024]{1,0:T(8,128)(2,1)} %all-gather.10.cloned.1.call-done) | copy-start | bytes 6291460
  1007.0 4.0 copy-start.9
  1007.0 5.0 copy-start.6
  1012.0 3.7 copy-start.5
  (3 other events, 1.9 us)
Sparse Core Ops, SparseCore 0:
  9.6 25.2 all-gather.9
  36.5 46.3 all-gather.7
  84.4 58.2 all-gather.11
  144.2 58.2 all-gather.13
  204.9 44.5 reduce-scatter.6
  251.9 99.5 reduce-scatter.4
  354.1 125.0 reduce-scatter.10
  481.8 125.0 reduce-scatter.8
  611.6 395.3 all-reduce.8
where the time goes:
time: 1030 us; the launch traced here: 1020 us
  waiting for transfers between devices  767 us (74%)
  matrix products  116 us (11%)
  blocking collectives  56.7 us (6%)
  local copies, waits for them, and re-layouts  50.1 us (5%)
  other arithmetic  18 us (2%)
  between operations  16.2 us (2%)
    psum x1, waiting for transfers between devices, body(): lax.psum((owner_sums[0], owner_sums[1], owner_sums[2], owner_sums[3], own...  325 us
    reduce_scatter x1, waiting for transfers between devices, body(): lax.psum_scatter(grad_in, 'shard', scatter_dimension=0, tiled=True)  128 us
    reduce_scatter x1, waiting for transfers between devices, body(): lax.psum_scatter(grad_fc, 'shard', scatter_dimension=0, tiled=True)  128 us
    reduce_scatter x1, waiting for transfers between devices, body(): lax.psum_scatter(grad_qkv, 'shard', scatter_dimension=0, tiled=True)  102 us
    all_gather x1, waiting for transfers between devices, body(): lax.all_gather(qkv_weight, 'shard', axis=0, tiled=True)  44.5 us
    psum x1, blocking collectives, body(): lax.psum((owner_sums[0], owner_sums[1], owner_sums[2], owner_sums[3], own...  23.6 us
    unnamed x96, local copies, waits for them, and re-layouts  23.1 us
    reduce_scatter x1, waiting for transfers between devices, body(): lax.psum_scatter(grad_out, 'shard', scatter_dimension=0, tiled=True)  22.9 us
  transfers between devices with their start and end apart: 9, of which 8 were waited for; matrix products, arithmetic and copies ran while one was open for 16% of the time, Pallas kernels for 0%

commit v1 on v0

--- a/solution.py
+++ b/solution.py
@@ -245,11 +245,11 @@
     rep_count = lax.axis_size("rep")
     shard_count = lax.axis_size("shard")
     grad_scale = 1.0 / math.sqrt(TOK_DEV * rep_count * shard_count)
-    grad_qkv = grad_qkv * grad_scale
-    grad_out = grad_out * grad_scale
-    grad_in = grad_in * grad_scale
+    grad_qkv = (grad_qkv * grad_scale).astype(jnp.bfloat16)
+    grad_out = (grad_out * grad_scale).astype(jnp.bfloat16)
+    grad_in = (grad_in * grad_scale).astype(jnp.bfloat16)
     grad_in_bias = grad_in_bias * grad_scale
-    grad_fc = grad_fc * grad_scale
+    grad_fc = (grad_fc * grad_scale).astype(jnp.bfloat16)
     grad_fc_bias = grad_fc_bias * grad_scale
     grad_gain = grad_gain * grad_scale
     grad_shift = grad_shift * grad_scale
@@ -279,11 +279,11 @@
     return (
         layer_out,
         input_grad,
-        summed[0],
-        summed[1],
-        summed[2],
+        summed[0].astype(jnp.float32),
+        summed[1].astype(jnp.float32),
+        summed[2].astype(jnp.float32),
         summed[3],
-        summed[4],
+        summed[4].astype(jnp.float32),
         summed[5],
         summed[6],
         summed[7],

time: 1030 us -> 685 us (0.67)
  waiting for transfers between devices: 767 us -> 422 us
  other arithmetic: 18 us -> 28.8 us
    psum x1, waiting for transfers between devices: 325 us -> 148 us  [body(): lax.psum((owner_sums[0], owner_sums[1], owner_sums[2], owner_sums[3], own...]
    reduce_scatter x1, waiting for transfers between devices: 128 us -> 74 us  [body(): lax.psum_scatter(grad_in, 'shard', scatter_dimension=0, tiled=True)]
    reduce_scatter x1, waiting for transfers between devices: 128 us -> 74 us  [body(): lax.psum_scatter(grad_fc, 'shard', scatter_dimension=0, tiled=True)]
    reduce_scatter x1, waiting for transfers between devices: 102 us -> 61.3 us  [body(): lax.psum_scatter(grad_qkv, 'shard', scatter_dimension=0, tiled=True)]
    reduce_scatter x1, waiting for transfers between devices: 22.9 us -> 3.86 us  [body(): lax.psum_scatter(grad_out, 'shard', scatter_dimension=0, tiled=True)]
    convert_element_type x0 -> x4, other arithmetic: none -> 10.7 us  [the longest x1 3.43 us: body(): summed[0].astype(jnp.float32)]
    unnamed x96 -> x90, local copies, waits for them, and re-layouts: 23.1 us -> 12.5 us
  transfers between devices with their start and end apart: 9 -> 9, of which waited for: 8 -> 8; matrix products, arithmetic and copies ran while one was open for 16% -> 24% of each run, Pallas kernels for 0% -> 0%
where the time goes in v1:
time: 685 us; the launch traced here: 679 us
  waiting for transfers between devices  422 us (62%)
  matrix products  113 us (16%)
  blocking collectives  57.6 us (8%)
  local copies, waits for them, and re-layouts  40.4 us (6%)
  other arithmetic  28.8 us (4%)
  between operations  16.2 us (2%)
    psum x1, waiting for transfers between devices, body(): lax.psum((owner_sums[0], owner_sums[1], owner_sums[2], owner_sums[3], own...  148 us
    reduce_scatter x1, waiting for transfers between devices, body(): lax.psum_scatter(grad_fc, 'shard', scatter_dimension=0, tiled=True)  74 us
    reduce_scatter x1, waiting for transfers between devices, body(): lax.psum_scatter(grad_in, 'shard', scatter_dimension=0, tiled=True)  74 us
    reduce_scatter x1, waiting for transfers between devices, body(): lax.psum_scatter(grad_qkv, 'shard', scatter_dimension=0, tiled=True)  61.3 us
    all_gather x1, waiting for transfers between devices, body(): lax.all_gather(qkv_weight, 'shard', axis=0, tiled=True)  44.5 us
    psum x1, blocking collectives, body(): lax.psum((owner_sums[0], owner_sums[1], owner_sums[2], owner_sums[3], own...  23.8 us
  transfers between devices with their start and end apart: 9, of which 8 were waited for; matrix products, arithmetic and copies ran while one was open for 24% of the time, Pallas kernels for 0%

profile of v1, /device:TPU:0, one launch (start us, length us, event | category | flops | bytes accessed | tf_op | source)
XLA Modules:
  0.0 679.0 jit_solution(2033070267634318230)
XLA Ops:
  12.2 6.0 all-gather.1
  18.2 5.4 all-gather
  25.1 9.9 %all-gather.10.cloned.1.call-done = bf16[1024,1024]{1,0:T(8,128)(2,1)} async-done(((bf16[256,1024]{1,0:T(8,128)(2,1)}), bf16[1024,1024]{1,0:T(8,128)(2,1)}) %all-gather.10.cloned.1.call-update) | async-done | bytes 2097168 | tf_op jit(solution)/shard_map/all_gather | solution.py:166
  35.0 2.9 convolution_convert_fusion
  38.4 44.5 %all-gather.8.cloned.1.call-done = bf16[1024,3072]{1,0:T(8,128)(2,1)} async-done(((bf16[256,3072]{1,0:T(8,128)(2,1)}), bf16[1024,3072]{1,0:T(8,128)(2,1)}) %all-gather.8.cloned.1.call-update) | async-done | bytes 6291472 | tf_op jit(solution)/shard_map/all_gather | solution.py:165
  82.9 5.7 fusion.98
  89.8 2.3 fusion.101
  92.1 3.2 copy.90
  95.3 2.4 slice.203
  97.7 2.3 slice.123
  100.0 2.9 copy.93
  102.9 2.1 slice.202
  105.0 2.3 slice.128
  119.4 2.3 multiply_reduce_fusion
  121.7 4.1 multiply_convert_fusion.3
  125.8 3.0 fusion.59
  128.8 2.3 multiply_reduce_fusion.1
  131.1 3.9 multiply_convert_fusion.4
  135.0 3.2 fusion.60
  144.0 2.7 multiply_convert_fusion.6
  146.7 3.7 fusion.57
  150.7 4.4 fusion.58
  164.2 8.8 %multiply_convert_fusion.2 = bf16[1024,3072]{1,0:T(8,128)(2,1)} fusion(bf16[512,1024]{0,1:T(8,128)(2,1)S(1)} %bitcast.90, bf16[512,1024]{0,1:T(8,128)(2,1)S(1)} %bitcast.88, bf16[512,1024]{0,1:T(8,128)(2,1)S(1)} %bitcast.86, bf16[512,1024]{1,0:T(8,128)(2,1)S(1)} %copy-done.2, f32[1024]{0:T(1024)S(1)} %bitcast.100, f32[1024]{0:T(1024)S(1)} %bitcast.93, ...), kind=kOutput, calls=%fused_computation.2 | convolution fusion | flops 3240099840 | bytes 10498048 | tf_op jit(solution)/shard_map/td,te->de/dot_general | solution.py:236
  173.6 5.8 all_gather.34
  179.4 7.2 %fusion.96 = f32[512,4096]{1,0:T(8,128)S(1)} fusion(bf16[1024,4096]{1,0:T(8,128)(2,1)} %all-gather.12.cloned.1.call-done, bf16[512,1024]{1,0:T(8,128)(2,1)S(1)} %copy-done.2, f32[1024]{0:T(1024)S(1)} %bitcast.101, f32[1024]{0:T(1024)S(1)} %bitcast.94, f32[512]{0:T(512)S(1)} %fusion.81, f32[512]{0:T(512)S(1)} %broadcast_multiply_fusion.5), kind=kOutput, calls=%fused_computation.164 | convolution fusion | flops 4298113024 | bytes 17838080 | tf_op jit(solution)/shard_map/dot_general | solution.py:192
  186.7 3.2 copy-done.35
  189.9 8.8 %multiply_convert_fusion = bf16[4096,1024]{1,0:T(8,128)(2,1)} fusion(bf16[512,1024]{1,0:T(8,128)(2,1)S(1)} %copy-done.18, bf16[512]{0:T(512)(128)(2,1)S(1)} %fusion.80, f32[512,4096]{1,0:T(8,128)S(1)} %fusion.96, f32[4096]{0:T(1024)S(1)} %convert_element_type.126), kind=kOutput, calls=%fused_computation | convolution fusion | flops 4324851712 | bytes 17843200 | tf_op jit(solution)/shard_map/tf,td->fd/dot_general | solution.py:211
  199.0 3.5 all-gather.14.cloned.1.call-done
  202.5 13.1 %convert_reduce_fusion = (f32[4096]{0:T(1024)S(1)}, bf16[512,4096]{1,0:T(8,128)(2,1)S(1)}) fusion(f32[512,4096]{1,0:T(8,128)} %copy-done.35, f32[4096]{0:T(1024)S(1)} %convert_element_type.126, bf16[4096,1024]{1,0:T(8,128)(2,1)} %all-gather.14.cloned.1.call-done, bf16[512,1024]{1,0:T(8,128)(2,1)S(1)} %copy-done.18, bf16[512]{0:T(512)(128)(2,1)S(1)} %fusion.80), kind=kOutput, calls=%fused_computation.12 | convolution fusion | flops 4343721984 | bytes 22053888 | tf_op jit(solution)/shard_map/td,fd->tf/dot_general | solution.py:214
  215.6 2.0 copy-done.36
  217.6 7.2 %multiply_convert_fusion.1 = bf16[1024,4096]{1,0:T(8,128)(2,1)} fusion(bf16[512,4096]{1,0:T(8,128)(2,1)S(1)} %get-tuple-element.57, bf16[512,1024]{1,0:T(8,128)(2,1)S(1)} %copy-done.2, f32[1024]{0:T(1024)S(1)} %bitcast.102, f32[1024]{0:T(1024)S(1)} %bitcast.95, f32[512]{0:T(512)S(1)} %fusion.81, f32[512]{0:T(512)S(1)} %broadcast_multiply_fusion.5), kind=kOutput, calls=%fused_computation.1 | convolution fusion | flops 4306501632 | bytes 13643776 | tf_op jit(solution)/shard_map/td,tf->df/dot_general | solution.py:217
  227.4 5.4 all-gather.2
  232.8 3.9 reduce-scatter.7.cloned.1.call-done
  236.7 61.3 %reduce-scatter.5.cloned.1.call-done = bf16[256,3072]{1,0:T(8,128)(2,1)} async-done(((bf16[1024,3072]{1,0:T(8,128)(2,1)}), bf16[256,3072]{1,0:T(8,128)(2,1)}) %reduce-scatter.5.cloned.1.call-update) | async-done | bytes 1572880 | tf_op jit(solution)/shard_map/reduce_scatter | solution.py:257
  297.9 74.0 %reduce-scatter.11.cloned.1.call-done = bf16[1024,1024]{1,0:T(8,128)(2,1)} async-done(((bf16[4096,1024]{1,0:T(8,128)(2,1)}), bf16[1024,1024]{1,0:T(8,128)(2,1)}) %reduce-scatter.11.cloned.1.call-update) | async-done | bytes 2097168 | tf_op jit(solution)/shard_map/reduce_scatter | solution.py:261
  372.0 74.0 %reduce-scatter.9.cloned.1.call-done = bf16[256,4096]{1,0:T(8,128)(2,1)} async-done(((bf16[1024,4096]{1,0:T(8,128)(2,1)}), bf16[256,4096]{1,0:T(8,128)(2,1)}) %reduce-scatter.9.cloned.1.call-update) | async-done | bytes 2097168 | tf_op jit(solution)/shard_map/reduce_scatter | solution.py:259
  446.0 8.4 %fusion.104 = f32[512,1024]{1,0:T(8,128)S(1)} fusion(bf16[512,4096]{1,0:T(8,128)(2,1)} %copy-done.36, bf16[1024,4096]{1,0:T(8,128)(2,1)} %all-gather.12.cloned.1.call-done), kind=kOutput, calls=%fused_computation.170 | convolution fusion | flops 4294967296 | bytes 14680064 | tf_op jit(solution)/shard_map/tf,df->td/dot_general | solution.py:239
  454.4 7.4 %fusion.100 = (f32[1024]{0:T(1024)S(1)}, f32[512]{0:T(512)S(1)}, f32[512,1024]{1,0:T(8,128)S(1)}) fusion(f32[1024]{0:T(1024)S(1)} %bitcast.96, f32[512]{0:T(512)S(1)} %broadcast_multiply_fusion.5, bf16[512,1024]{1,0:T(8,128)(2,1)S(1)} %copy-done.2, f32[512,1024]{1,0:T(8,128)S(1)} %fusion.104, bf16[1024,3072]{1,0:T(8,128)(2,1)} %all-gather.8.cloned.1.call-done, ...), kind=kOutput, calls=%fused_computation.166 | convolution fusion | flops 3234331136 | bytes 14692352 | tf_op jit(solution)/shard_map/te,de->td/dot_general | solution.py:237
  462.9 1.9 convert_reduce_fusion.2
  464.9 11.1 %all-reduce.5 = (f32[4096]{0:T(1024)S(1)}, f32[1024]{0:T(1024)S(1)}, f32[1024]{0:T(1024)S(1)}, f32[1024]{0:T(1024)S(1)}) all-reduce(f32[4096]{0:T(1024)S(1)} %broadcast_multiply_fusion.1, f32[1024]{0:T(1024)S(1)} %broadcast_multiply_fusion.4, ...), channel_id=5, replica_groups=mesh['rep'=8,'shard'=4] {'shard'}, use_global_device_ids=true, to_apply=%region_20.21.clone | all-reduce | flops 7168 | bytes 57344
  476.2 23.8 %all-reduce.4 = (f32[1024]{0:T(1024)}, f32[256]{0:T(256)}, f32[256]{0:T(256)}, f32[256]{0:T(256)}) all-reduce(f32[1024]{0:T(1024)S(1)} %dynamic-slice.1, f32[256]{0:T(256)S(1)} %dynamic-slice.3, f32[256]{0:T(256)S(1)} %dynamic-slice.5, f32[256]{0:T(256)S(1)} %dynamic-slice.7), channel_id=1, replica_groups=mesh['rep'=8,'shard'=4] {'rep'}, use_global_device_ids=true, to_apply=%region_21.22 | all-reduce | flops 1792 | bytes 14336 | tf_op jit(solution)/shard_map/psum | solution.py:266
  500.0 10.6 %fusion.93 = f32[512,1024]{1,0:T(8,128)S(1)} fusion(bf16[4096,1024]{1,0:T(8,128)(2,1)} %all-gather.14.cloned.1.call-done, f32[512,4096]{1,0:T(8,128)} %copy-done.35, f32[4096]{0:T(1024)S(1)} %convert_element_type.126), kind=kOutput, calls=%fused_computation.163 | convolution fusion | flops 4315938816 | bytes 18890752 | tf_op jit(solution)/shard_map/dot_general | solution.py:197
  510.7 2.4 fusion.32
  513.1 148.5 %all-reduce.9.cloned.1.call-done = (bf16[256,3072]{1,0:T(8,128)(2,1)}, bf16[256,1024]{1,0:T(8,128)(2,1)}, bf16[256,4096]{1,0:T(8,128)(2,1)}, bf16[1024,1024]{1,0:T(8,128)(2,1)}) async-done(((bf16[256,3072]{1,0:T(8,128)(2,1)}, bf16[256,1024]{1,0:T(8,128)(2,1)}, bf16[256,4096]{1,0:T(8,128)(2,1)}, bf16[1024,1024]{1,0:T(8,128)(2,1)}), (bf16[256,3072]{1,0:T(8,128)(2,1)}, bf16[256,1024]{1,0:T(8,128)(2,1)}, ...) | async-done | bytes 6291472 | tf_op jit(solution)/shard_map/psum | solution.py:266
  661.5 2.3 convert_element_type.142
  663.8 3.4 convert_element_type.140
  667.2 2.5 convert_element_type.144
  669.7 2.5 convert_element_type.147
  (168 shorter events, 38.5 us)
Async XLA Ops:
  7.2 2.9 copy-start.29
  7.2 3.0 copy-start.28
  7.2 4.2 copy-start.31
  7.2 4.3 copy-start.32
  7.2 4.3 copy-start.27
  7.2 4.3 copy-start.2
  7.2 27.7 %all-gather.10.cloned.1.call-start = ((), (), s32[]{:S(2)}) async-start(), calls=%async_computation.5 | async-start | bytes 2621440 | tf_op jit(solution)/shard_map/all_gather | solution.py:166
  8.0 27.0 %copy-start.16 = (bf16[512,1024]{1,0:T(8,128)(2,1)S(1)}, bf16[512,1024]{1,0:T(8,128)(2,1)}, u32[]{:S(2)}) copy-start(bf16[512,1024]{1,0:T(8,128)(2,1)} %param.25) | copy-start | bytes 3145732
  8.0 74.9 %all-gather.8.cloned.1.call-start = ((), (), s32[]{:S(2)}) async-start(), calls=%async_computation.4 | async-start | bytes 7864320 | tf_op jit(solution)/shard_map/all_gather | solution.py:165
  8.7 170.7 %all-gather.12.cloned.1.call-start = ((), (), s32[]{:S(2)}) async-start(), calls=%async_computation.6 | async-start | bytes 10485760 | tf_op jit(solution)/shard_map/all_gather | solution.py:167
  9.5 193.0 %all-gather.14.cloned.1.call-start = ((), (), s32[]{:S(2)}) async-start(), calls=%async_computation.7 | async-start | bytes 10485760 | tf_op jit(solution)/shard_map/all_gather | solution.py:169
  10.0 226.6 %reduce-scatter.7.cloned.1.call-start = ((), (), s32[]{:S(2)}) async-start(), calls=%async_computation.9 | async-start | bytes 2621440 | tf_op jit(solution)/shard_map/reduce_scatter | solution.py:258
  12.1 11.4 %copy-start.24 = (f32[512]{0:T(512)}, f32[512]{0:T(512)S(1)}, u32[]{:S(2)}) copy-start(f32[512]{0:T(512)S(1)} %fusion.29) | copy-start | bytes 6148
  112.6 1.1 copy-start.19
  112.6 1.2 copy-start.22
  113.4 3.2 copy-start.21
  113.8 12.0 %copy-start.23 = (bf16[512,16,32]{0,2,1:T(8,128)(2,1)}, bf16[512,16,32]{0,2,1:T(8,128)(2,1)S(1)}, u32[]{:S(2)}) copy-start(bf16[512,16,32]{0,2,1:T(8,128)(2,1)S(1)} %copy.120) | copy-start | bytes 1572868
  115.4 24.4 %copy-start = (f32[8,512,512]{1,2,0:T(8,128)}, f32[8,512,512]{1,2,0:T(8,128)S(1)}, u32[]{:S(2)}) copy-start(f32[8,512,512]{1,2,0:T(8,128)S(1)} %get-tuple-element.50) | copy-start | bytes 25165828
  118.2 23.1 %copy-start.1 = (f32[8,512,512]{1,2,0:T(8,128)}, f32[8,512,512]{1,2,0:T(8,128)S(1)}, u32[]{:S(2)}) copy-start(f32[8,512,512]{1,2,0:T(8,128)S(1)} %get-tuple-element.48) | copy-start | bytes 25165828
  128.8 9.3 %copy-start.6 = (bf16[512,8,64]{0,2,1:T(8,128)(2,1)}, bf16[512,8,64]{0,2,1:T(8,128)(2,1)S(1)}, u32[]{:S(2)}) copy-start(bf16[512,8,64]{0,2,1:T(8,128)(2,1)S(1)} %fusion.59) | copy-start | bytes 1572868
  138.1 3.2 copy-start.8
  141.4 2.6 copy-start.17
  143.0 1.0 copy-start.10
  144.0 2.7 copy-start.20
  150.3 147.6 %reduce-scatter.5.cloned.1.call-start = ((), (), s32[]{:S(2)}) async-start(), calls=%async_computation.8 | async-start | bytes 7864320 | tf_op jit(solution)/shard_map/reduce_scatter | solution.py:257
  150.6 5.2 copy-start.3
  155.1 2.9 slice-start
  155.8 1.7 copy-start.7
  155.8 1.9 copy-start.9
  156.2 3.6 slice-start.1
  157.8 6.3 copy-start.12
  157.8 3.4 slice-start.2
  159.8 4.4 copy-start.14
  159.8 2.9 slice-start.3
  173.0 199.0 %reduce-scatter.11.cloned.1.call-start = ((), (), s32[]{:S(2)}) async-start(), calls=%async_computation.11 | async-start | bytes 10485760 | tf_op jit(solution)/shard_map/reduce_scatter | solution.py:261
  179.4 10.5 %copy-start.18 = (bf16[512,1024]{1,0:T(8,128)(2,1)S(1)}, bf16[512,1024]{1,0:T(8,128)(2,1)}, u32[]{:S(2)}) copy-start(bf16[512,1024]{1,0:T(8,128)(2,1)} %param.25) | copy-start | bytes 3145732
  186.7 3.2 copy-start.35
  198.8 247.2 %reduce-scatter.9.cloned.1.call-start = ((), (), s32[]{:S(2)}) async-start(), calls=%async_computation.10 | async-start | bytes 10485760 | tf_op jit(solution)/shard_map/reduce_scatter | solution.py:259
  215.6 2.0 copy-start.36
  224.8 2.5 copy-start.33
  224.9 436.7 %all-reduce.9.cloned.1.call-start = ((), (), s32[]{:S(2)}) async-start(), calls=%async_computation.12 | async-start | bytes 12582912 | tf_op jit(solution)/shard_map/psum | solution.py:266
  446.0 8.4 %copy-start.13 = (bf16[512,16,64]{0,2,1:T(8,128)(2,1)S(1)}, bf16[512,16,64]{0,2,1:T(8,128)(2,1)}, u32[]{:S(2)}) copy-start(bf16[512,16,64]{0,2,1:T(8,128)(2,1)} %copy-done.12) | copy-start | bytes 3145732
  446.0 8.4 %copy-start.15 = (bf16[512,16,64]{0,2,1:T(8,128)(2,1)S(1)}, bf16[512,16,64]{0,2,1:T(8,128)(2,1)}, u32[]{:S(2)}) copy-start(bf16[512,16,64]{0,2,1:T(8,128)(2,1)} %copy-done.14) | copy-start | bytes 3145732
  454.4 7.5 %copy-start.25 = (f32[512]{0:T(512)S(1)}, f32[512]{0:T(512)}, u32[]{:S(2)}) copy-start(f32[512]{0:T(512)} %copy-done.24) | copy-start | bytes 6148
  500.0 10.6 %copy-start.11 = (bf16[512,16,64]{0,2,1:T(8,128)(2,1)S(1)}, bf16[512,16,64]{0,2,1:T(8,128)(2,1)}, u32[]{:S(2)}) copy-start(bf16[512,16,64]{0,2,1:T(8,128)(2,1)} %copy-done.10) | copy-start | bytes 3145732
  500.0 10.6 %copy-start.30 = (bf16[1024,1024]{1,0:T(8,128)(2,1)S(1)}, bf16[1024,1024]{1,0:T(8,128)(2,1)}, u32[]{:S(2)}) copy-start(bf16[1024,1024]{1,0:T(8,128)(2,1)} %all-gather.10.cloned.1.call-done) | copy-start | bytes 6291460
  661.5 5.7 copy-start.5
  667.2 2.5 copy-start.4
  (2 other events, 1.3 us)
Sparse Core Ops, SparseCore 0:
  9.6 25.2 all-gather.9
  36.5 46.3 all-gather.7
  84.5 58.2 all-gather.11
  144.2 58.2 all-gather.13
  205.5 31.1 reduce-scatter.6
  239.1 58.8 reduce-scatter.4
  300.5 71.3 reduce-scatter.10
  374.5 71.3 reduce-scatter.8
  450.4 211.0 all-reduce.8
